TPU v7x, 512 devices: a whole 4x4x16 slice. The times are simulated.
512 devices in a mesh: walk: 64 (over z, y), col: 8 (over x, core).
Axes of the slice: x: 4, y: 4, z: 16, core: 2. Of those that a mesh axis runs over, the one named last changes fastest.
Arguments:
- jacobian: float32 [384, 524288], P('walk', 'col'), may hold values from -25 to 25
- prev_update: float32 [8, 65536], P('col', 'walk'), may hold values from -6 to 6
- base_energy: float32 [384], P('walk'), may hold values from -6 to 6
- elec_pos: float32 [384, 3, 66], P('walk'), may hold values from -8 to 8
- atom_pos: float32 [3, 21], replicated, may hold values from -6 to 6
- quad_ratio: float32 [384, 21, 66, 12], P('walk'), may hold values from -1.2 to 1.2
- rotation: int32 [384, 66], P('walk'), may hold values from 0 to 15
- channels: int32 [21], replicated, may hold values from 1 to 3
- ecp_coef: float32 [21, 3], replicated, may hold values from 0.5 to 2
- ecp_expo: float32 [21, 3], replicated, may hold values from 0.2 to 2
Outputs:
- local_energy: float32 [384], P('walk')
- update: float32 [8, 65536], P('col', 'walk')
All inputs are finite; a program needn't handle non-finite values.
Results may differ from a plain program's by a relative error of at most 0.0003.
Values sent between devices are 32-bit elements; how exact they have to be, the bound alone decides.
No kernel may reach another device: no remote copies, remote signals or barrier semaphores. Data moves between devices by JAX's collectives and lax.ppermute only.
A program may use at most 64 MiB of HBM per device.

v0:
```python
import math
import jax
import jax.numpy as jnp
from jax import lax
from jax.sharding import PartitionSpec as P

NROT = 16
momentum = 0.9
damping = 0.1


def icosa_points():
    golden = (1.0 + math.sqrt(5.0)) / 2.0
    length = math.sqrt(1.0 + golden * golden)
    rows = []
    for first in (-1.0, 1.0):
        for second in (-golden, golden):
            rows.append((0.0, first / length, second / length))
            rows.append((first / length, second / length, 0.0))
            rows.append((second / length, 0.0, first / length))
    return jnp.asarray(rows, dtype=jnp.float32).T


def rotation_table(count):
    angle = jnp.arange(count, dtype=jnp.float32)
    turn_z = 2.0 * math.pi * angle / count
    turn_x = 0.9 * angle
    cz, sz = (jnp.cos(turn_z), jnp.sin(turn_z))
    cx, sx = (jnp.cos(turn_x), jnp.sin(turn_x))
    zeros = jnp.zeros_like(cz)
    matrix = jnp.stack(
        [
            jnp.stack([cz, -sz * cx, sz * sx], axis=-1),
            jnp.stack([sz, cz * cx, -cz * sx], axis=-1),
            jnp.stack([zeros, sx, cx], axis=-1),
        ],
        axis=1,
    )
    points = icosa_points()
    rotated = matrix[:, :, 0, None] * points[None, 0, :]
    rotated = rotated + matrix[:, :, 1, None] * points[None, 1, :]
    rotated = rotated + matrix[:, :, 2, None] * points[None, 2, :]
    return rotated.reshape(count, -1)


def nonlocal_energy(elec_pos, atom_pos, quad_ratio, rotation, channels, ecp_coef, ecp_expo):
    walkers, electrons = rotation.shape
    count = NROT
    table = rotation_table(count)
    onehot = (rotation[:, :, None] == jnp.arange(count, dtype=jnp.int32)[None, None, :]).astype(
        jnp.float32
    )
    rotated = jnp.einsum("wek,kf->wef", onehot, table, precision=lax.Precision.HIGHEST)
    rotated = rotated.reshape(walkers, electrons, 3, -1)
    diff = elec_pos[:, :, None, :] - atom_pos[None, :, :, None]
    dist2 = jnp.sum(diff * diff, axis=1)
    unit = diff / jnp.sqrt(dist2 + 0.01)[:, None, :, :]
    cosang = unit[:, 0, :, :, None] * rotated[:, None, :, 0, :]
    cosang = cosang + unit[:, 1, :, :, None] * rotated[:, None, :, 1, :]
    cosang = cosang + unit[:, 2, :, :, None] * rotated[:, None, :, 2, :]
    quad = quad_ratio.shape[-1]
    lmax = ecp_coef.shape[1]
    lower = jnp.ones_like(cosang)
    upper = cosang
    total = jnp.zeros((walkers,), jnp.float32)
    for level in range(lmax):
        if level == 0:
            poly = lower
        elif level == 1:
            poly = upper
        else:
            fresh = ((2 * level - 1) * cosang * upper - (level - 1) * lower) / level
            lower, upper = (upper, fresh)
            poly = fresh
        angular = jnp.sum(poly * quad_ratio, axis=-1) / quad
        active = (channels > level).astype(jnp.float32)
        radial = ecp_coef[None, :, level, None] * jnp.exp(-ecp_expo[None, :, level, None] * dist2)
        term = (2 * level + 1) * active[None, :, None] * radial * angular
        total = total + jnp.sum(term, axis=(1, 2))
    return total


def sum_pieces(first, second):
    first_sum, second_sum = lax.psum((first, second), ("walk", "col"))
    return (first_sum, second_sum)


def body(
    jacobian,
    prev_update,
    base_energy,
    elec_pos,
    atom_pos,
    quad_ratio,
    rotation,
    channels,
    ecp_coef,
    ecp_expo,
):
    energy_mine = base_energy + nonlocal_energy(
        elec_pos, atom_pos, quad_ratio, rotation, channels, ecp_coef, ecp_expo
    )
    columns = lax.all_to_all(jacobian, "walk", split_axis=1, concat_axis=0, tiled=True)
    walkers = columns.shape[0]
    params_total = columns.shape[1] * lax.axis_size("walk") * lax.axis_size("col")
    scale = 1.0 / params_total
    centred = columns - jnp.mean(columns, axis=0, keepdims=True)
    prev_mine = prev_update[0]
    gram_part = (
        jnp.dot(
            centred, centred.T, precision=lax.Precision.HIGHEST, preferred_element_type=jnp.float32
        )
        * scale
    )
    along_part = (
        jnp.dot(
            centred, prev_mine, precision=lax.Precision.HIGHEST, preferred_element_type=jnp.float32
        )
        * scale
    )
    extra = along_part[:, None]
    gram, extra_sum = sum_pieces(gram_part, extra)
    along = extra_sum[:, 0]
    energies = lax.all_gather(energy_mine, "walk", axis=0, tiled=True)
    eps = -(energies - jnp.mean(energies)) / math.sqrt(walkers)
    system = gram + damping * jnp.eye(walkers, dtype=jnp.float32)
    factor = jnp.linalg.cholesky(system)
    solved = jax.scipy.linalg.cho_solve((factor, True), eps - momentum * along)
    update_mine = (
        jnp.dot(
            solved, centred, precision=lax.Precision.HIGHEST, preferred_element_type=jnp.float32
        )
        + momentum * prev_mine
    )
    return (energy_mine, update_mine[None, :])


def solution(mesh):
    in_specs = (
        P("walk", "col"),
        P("col", "walk"),
        P("walk"),
        P("walk", None, None),
        P(),
        P("walk", None, None, None),
        P("walk", None),
        P(),
        P(),
        P(),
    )
    out_specs = (P("walk"), P("col", "walk"))
    return jax.shard_map(body, mesh=mesh, in_specs=in_specs, out_specs=out_specs, check_vma=False)
```

profile of v0, /device:TPU:1, one launch (start us, length us, event | category | flops | bytes accessed | tf_op | source)
XLA Modules:
  0.0 826.4 jit_solution(6028116304954348564)
XLA Ops:
  7.3 19.4 %all-to-all-start = ((f32[6,64,1024]{2,0,1:T(8,128)}), f32[6,64,1024]{2,0,1:T(8,128)S(1)}, u32[]{:S(2)}, u32[]{:S(2)}) async-start(f32[6,64,1024]{2,0,1:T(8,128)} %bitcast.162), calls=%async_computation | async-start | bytes 4194304 | tf_op jit(solution)/shard_map/all_to_all | solution.py:103
  28.4 1.3 dynamic-slice.3
  30.9 0.6 multiply_reduce_fusion
  31.8 0.5 fusion.57
  32.3 187.9 %all-reduce.1 = f32[384]{0:T(512)S(1)} all-reduce(f32[384]{0:T(512)S(1)} %get-tuple-element.32), channel_id=1, replica_groups=mesh['walk'=64,'col'=8] {'walk'}, use_global_device_ids=true, to_apply=%add.1 | all-reduce | flops 384 | bytes 3072
  220.3 0.6 reduce_sum.89
  221.7 1.6 subtract_bitcast_fusion
  223.3 1.6 sub.49
  225.0 3.4 convolution_multiply_fusion
  228.4 1.4 convolution_reduce_fusion
  229.9 133.3 %psum.15 = f32[384,1]{0,1:T(1,128)S(1)} all-reduce(f32[384,1]{0,1:T(1,128)S(1)} %broadcast_in_dim.6), channel_id=1, replica_groups=mesh['walk'=64,'col'=8] {'walk','col'}, use_global_device_ids=true, to_apply=%region_16.17 | all-reduce | flops 384 | bytes 3072 | tf_op jit(solution)/shard_map/psum | solution.py:84
  363.3 355.0 %all-reduce.4.cloned.1.call-done = f32[384,384]{0,1:T(8,128)} async-done(((f32[384,384]{0,1:T(8,128)}), f32[384,384]{0,1:T(8,128)}) %all-reduce.4.cloned.1.call-update) | async-done | bytes 589840 | tf_op jit(solution)/shard_map/psum | solution.py:84
  718.2 1.2 select_add_fusion
  719.8 11.7 %cholesky.76 = f32[128,128]{1,0:T(8,128)S(1)} custom-call(f32[128,128]{1,0:T(8,128)S(1)} %cholesky.189), custom_call_target="Cholesky" | custom-call | tf_op jit(solution)/shard_map/jit(cholesky)/cholesky | solution.py:127
  731.5 9.8 %custom-call.26 = f32[1,128,128]{1,2,0:T(8,128)S(1)} custom-call(f32[1,128,128]{2,1,0:T(8,128)S(1)} %get-tuple-element.45), custom_call_target="InvertDiagBlocksLowerTriangular" | custom-call | tf_op jit(solution)/shard_map/jit(cholesky)/cholesky | solution.py:127
  742.1 11.7 %cholesky.160 = f32[128,128]{1,0:T(8,128)S(1)} custom-call(f32[128,128]{1,0:T(8,128)S(1)} %cholesky.193), custom_call_target="Cholesky" | custom-call | tf_op jit(solution)/shard_map/jit(cholesky)/cholesky | solution.py:127
  754.0 10.0 %custom-call.27 = f32[1,128,128]{1,2,0:T(8,128)S(1)} custom-call(f32[1,128,128]{2,1,0:T(8,128)S(1)} %get-tuple-element.43), custom_call_target="InvertDiagBlocksLowerTriangular" | custom-call | tf_op jit(solution)/shard_map/jit(cholesky)/cholesky | solution.py:127
  764.0 0.3 convolution_dynamic-update-slice_fusion
  764.3 0.4 convolution_subtract_fusion.1
  764.7 11.7 %cholesky.179 = f32[128,128]{1,0:T(8,128)S(1)} custom-call(f32[128,128]{1,0:T(8,128)S(1)} %convolution_subtract_fusion.1), custom_call_target="Cholesky" | custom-call | tf_op jit(solution)/shard_map/jit(cholesky)/cholesky | solution.py:127
  776.6 0.7 compare_reduce_fusion
  777.3 0.6 compare_reduce_fusion.1
  779.9 6.7 while.1
  780.0 0.6 fusion.71
  780.6 1.4 dynamic-slice.8
  782.2 0.6 fusion.71
  782.8 1.4 dynamic-slice.8
  784.4 0.6 fusion.71
  785.0 1.4 dynamic-slice.8
  786.6 29.5 %custom-call.28 = f32[3,128,128]{1,2,0:T(8,128)S(1)} custom-call(f32[3,128,128]{2,1,0:T(8,128)S(1)} %get-tuple-element.9), custom_call_target="InvertDiagBlocksLowerTriangular" | custom-call | tf_op jit(solution)/shard_map/jit(_cho_solve)/triangular_solve | solution.py:128
  818.0 0.9 fusion.33
  818.9 0.6 multiply_add_fusion.1
  (115 shorter events, 6.6 us)
Async XLA Ops:
  7.2 20.8 %copy-start.11 = (f32[12]{0:T(128)S(1)}, f32[12]{0:T(128)}, u32[]{:S(2)}) copy-start(f32[12]{0:T(128)} %constant.198) | copy-start | bytes 148
  7.2 20.9 %copy-start.10 = (f32[12]{0:T(128)S(1)}, f32[12]{0:T(128)}, u32[]{:S(2)}) copy-start(f32[12]{0:T(128)} %constant.200) | copy-start | bytes 148
  7.2 20.9 %copy-start.9 = (f32[12]{0:T(128)S(1)}, f32[12]{0:T(128)}, u32[]{:S(2)}) copy-start(f32[12]{0:T(128)} %constant.202) | copy-start | bytes 148
  7.2 21.2 %copy-start.3 = (f32[6,3,66]{2,1,0:T(4,128)S(1)}, f32[6,3,66]{2,1,0:T(4,128)}, u32[]{:S(2)}) copy-start(f32[6,3,66]{2,1,0:T(4,128)} %param.14) | copy-start | bytes 14260
  7.2 23.1 %copy-start.4 = (f32[3,21]{1,0:T(4,128)S(1)}, f32[3,21]{1,0:T(4,128)}, u32[]{:S(2)}) copy-start(f32[3,21]{1,0:T(4,128)} %param.15) | copy-start | bytes 760
  7.2 23.2 %copy-start.12 = (s32[21]{0:T(128)S(1)}, s32[21]{0:T(128)}, u32[]{:S(2)}) copy-start(s32[21]{0:T(128)} %param.18) | copy-start | bytes 256
  7.2 23.3 %copy-start.6 = (f32[21,3]{0,1:T(4,128)S(1)}, f32[21,3]{0,1:T(4,128)}, u32[]{:S(2)}) copy-start(f32[21,3]{0,1:T(4,128)} %param.20) | copy-start | bytes 760
  7.2 23.3 %copy-start.7 = (f32[21,3]{0,1:T(4,128)S(1)}, f32[21,3]{0,1:T(4,128)}, u32[]{:S(2)}) copy-start(f32[21,3]{0,1:T(4,128)} %param.19) | copy-start | bytes 760
  7.3 23.3 %copy-start.5 = (s32[6,66]{1,0:T(8,128)S(1)}, s32[6,66]{1,0:T(8,128)}, u32[]{:S(2)}) copy-start(s32[6,66]{1,0:T(8,128)} %param.17) | copy-start | bytes 4756
  7.3 214.3 %all-to-all-start = ((f32[6,64,1024]{2,0,1:T(8,128)}), f32[6,64,1024]{2,0,1:T(8,128)S(1)}, u32[]{:S(2)}, u32[]{:S(2)}) async-start(f32[6,64,1024]{2,0,1:T(8,128)} %bitcast.162), calls=%async_computation | async-start | bytes 4194304 | tf_op jit(solution)/shard_map/all_to_all | solution.py:103
  26.7 4.2 copy-start.1
  26.7 691.5 %all-reduce.4.cloned.1.call-start = ((), (), s32[]{:S(2)}) async-start(), calls=%async_computation.1 | async-start | bytes 1179648 | tf_op jit(solution)/shard_map/psum | solution.py:84
  30.5 1.2 copy-start.8
  225.0 3.5 copy-start.2
  718.2 1.4 copy-start
Sparse Core Ops, SparseCore 0:
  228.5 489.6 all-reduce.3
where the time goes:
time: 827 us; the launch traced here: 826 us
  waiting for transfers between devices  355 us (43%)
  blocking collectives  321 us (39%)
  other arithmetic  92.2 us (11%)
  starting transfers between devices  19.5 us (2%)
  between operations  17.8 us (2%)
  local copies, waits for them, and re-layouts  11.5 us (1%)
  matrix products  9.1 us (1%)
    psum x1, waiting for transfers between devices, sum_pieces(): first_sum, second_sum = lax.psum((first, second), ('walk', 'col'))  355 us
    unnamed x1, blocking collectives  188 us
    psum x1, blocking collectives, sum_pieces(): first_sum, second_sum = lax.psum((first, second), ('walk', 'col'))  133 us
    another operation x10, other arithmetic, body(): factor = jnp.linalg.cholesky(system)  56.4 us
    another operation x3, other arithmetic, body(): solved = jax.scipy.linalg.cho_solve((factor, True), eps - momentum * along)  29.5 us
    all_to_all x1, starting transfers between devices, body(): lax.all_to_all(jacobian, 'walk', split_axis=1, concat_axis=0, tiled=True)  19.4 us
  transfers between devices with their start and end apart: 2, of which 1 were waited for; matrix products, arithmetic and copies ran while one was open for 1% of the time, Pallas kernels for 0%

commit v1 on v0

--- a/solution.py
+++ b/solution.py
@@ -7,6 +7,14 @@
 NROT = 16
 momentum = 0.9
 damping = 0.1
+
+
+def cover_tails(m):
+    odd = lax.axis_size("walk")
+    field_out = jnp.split(m, odd, axis=1)
+    arr_next = jnp.stack(field_out)
+    answer = lax.all_to_all(arr_next, axis_name="walk", split_axis=0, concat_axis=0)
+    return jnp.concatenate(answer, 0)
 
 
 def icosa_points():
@@ -100,7 +108,7 @@
     energy_mine = base_energy + nonlocal_energy(
         elec_pos, atom_pos, quad_ratio, rotation, channels, ecp_coef, ecp_expo
     )
-    columns = lax.all_to_all(jacobian, "walk", split_axis=1, concat_axis=0, tiled=True)
+    columns = cover_tails(jacobian)
     walkers = columns.shape[0]
     params_total = columns.shape[1] * lax.axis_size("walk") * lax.axis_size("col")
     scale = 1.0 / params_total

time: 827 us -> 918 us (1.11)
  local copies, waits for them, and re-layouts: 11.5 us -> 98.6 us
    unnamed x29 -> x92, local copies, waits for them, and re-layouts: 1.34 us -> 87.1 us
where the time goes in v1:
time: 918 us; the launch traced here: 914 us
  waiting for transfers between devices  355 us (39%)
  blocking collectives  321 us (35%)
  local copies, waits for them, and re-layouts  98.6 us (11%)
  other arithmetic  92.2 us (10%)
  starting transfers between devices  19.5 us (2%)
  between operations  17.8 us (2%)
    psum x1, waiting for transfers between devices, sum_pieces(): first_sum, second_sum = lax.psum((first, second), ('walk', 'col'))  355 us
    unnamed x1, blocking collectives  188 us
    psum x1, blocking collectives, sum_pieces(): first_sum, second_sum = lax.psum((first, second), ('walk', 'col'))  133 us
    unnamed x92, local copies, waits for them, and re-layouts  87.1 us
    another operation x10, other arithmetic, body(): factor = jnp.linalg.cholesky(system)  56.4 us
    another operation x3, other arithmetic, body(): solved = jax.scipy.linalg.cho_solve((factor, True), eps - momentum * along)  29.5 us
    all_to_all x1, starting transfers between devices, cover_tails(): lax.all_to_all(arr_next, axis_name='walk', split_axis=0, concat_axis=0)  19.4 us
  transfers between devices with their start and end apart: 2, of which 1 were waited for; matrix products, arithmetic and copies ran while one was open for 1% of the time, Pallas kernels for 0%

profile of v1, /device:TPU:1, one launch (start us, length us, event | category | flops | bytes accessed | tf_op | source)
XLA Modules:
  0.0 913.6 jit_solution(14875431696284601700)
XLA Ops:
  14.0 1.4 constant_dynamic-update-slice_fusion.58
  16.7 1.4 constant_dynamic-update-slice_fusion.56
  20.8 1.4 constant_dynamic-update-slice_fusion.53
  22.2 1.4 constant_dynamic-update-slice_fusion.52
  30.3 1.4 constant_dynamic-update-slice_fusion.46
  33.1 1.4 constant_dynamic-update-slice_fusion.44
  35.8 1.4 constant_dynamic-update-slice_fusion.42
  48.0 1.4 constant_dynamic-update-slice_fusion.33
  52.1 1.4 constant_dynamic-update-slice_fusion.30
  53.5 1.4 constant_dynamic-update-slice_fusion.29
  57.6 1.4 constant_dynamic-update-slice_fusion.26
  60.3 1.4 constant_dynamic-update-slice_fusion.24
  68.5 1.4 constant_dynamic-update-slice_fusion.18
  93.0 1.4 constant_dynamic-update-slice_fusion
  94.4 19.4 %all-to-all-start = ((f32[64,6,1024]{2,1,0:T(8,128)}), f32[64,6,1024]{2,1,0:T(8,128)S(1)}, u32[]{:S(2)}, u32[]{:S(2)}) async-start(f32[64,6,1024]{2,1,0:T(8,128)} %constant_dynamic-update-slice_fusion), calls=%async_computation | async-start | bytes 4194304 | tf_op jit(solution)/shard_map/all_to_all | solution.py:16
  119.5 188.0 %all-reduce.1 = f32[384]{0:T(512)S(1)} all-reduce(f32[384]{0:T(512)S(1)} %get-tuple-element.32), channel_id=1, replica_groups=mesh['walk'=64,'col'=8] {'walk'}, use_global_device_ids=true, to_apply=%add.1 | all-reduce | flops 384 | bytes 3072
  308.9 1.6 broadcast_subtract_fusion
  310.5 1.6 sub.45
  312.1 3.4 convolution_multiply_fusion
  315.6 1.4 convolution_reduce_fusion
  317.1 133.2 %psum.15 = f32[384,1]{0,1:T(1,128)S(1)} all-reduce(f32[384,1]{0,1:T(1,128)S(1)} %broadcast_in_dim.6), channel_id=1, replica_groups=mesh['walk'=64,'col'=8] {'walk','col'}, use_global_device_ids=true, to_apply=%region_16.17 | all-reduce | flops 384 | bytes 3072 | tf_op jit(solution)/shard_map/psum | solution.py:92
  450.3 355.2 %all-reduce.4.cloned.1.call-done = f32[384,384]{0,1:T(8,128)} async-done(((f32[384,384]{0,1:T(8,128)}), f32[384,384]{0,1:T(8,128)}) %all-reduce.4.cloned.1.call-update) | async-done | bytes 589840 | tf_op jit(solution)/shard_map/psum | solution.py:92
  807.0 11.7 %cholesky.76 = f32[128,128]{1,0:T(8,128)S(1)} custom-call(f32[128,128]{1,0:T(8,128)S(1)} %cholesky.189), custom_call_target="Cholesky" | custom-call | tf_op jit(solution)/shard_map/jit(cholesky)/cholesky | solution.py:135
  818.8 9.8 %custom-call.26 = f32[1,128,128]{1,2,0:T(8,128)S(1)} custom-call(f32[1,128,128]{2,1,0:T(8,128)S(1)} %get-tuple-element.45), custom_call_target="InvertDiagBlocksLowerTriangular" | custom-call | tf_op jit(solution)/shard_map/jit(cholesky)/cholesky | solution.py:135
  829.3 11.7 %cholesky.160 = f32[128,128]{1,0:T(8,128)S(1)} custom-call(f32[128,128]{1,0:T(8,128)S(1)} %cholesky.193), custom_call_target="Cholesky" | custom-call | tf_op jit(solution)/shard_map/jit(cholesky)/cholesky | solution.py:135
  841.2 10.0 %custom-call.27 = f32[1,128,128]{1,2,0:T(8,128)S(1)} custom-call(f32[1,128,128]{2,1,0:T(8,128)S(1)} %get-tuple-element.43), custom_call_target="InvertDiagBlocksLowerTriangular" | custom-call | tf_op jit(solution)/shard_map/jit(cholesky)/cholesky | solution.py:135
  852.0 11.7 %cholesky.179 = f32[128,128]{1,0:T(8,128)S(1)} custom-call(f32[128,128]{1,0:T(8,128)S(1)} %convolution_subtract_fusion.1), custom_call_target="Cholesky" | custom-call | tf_op jit(solution)/shard_map/jit(cholesky)/cholesky | solution.py:135
  867.1 6.7 while.1
  867.8 1.4 dynamic-slice.8
  870.1 1.4 dynamic-slice.8
  872.3 1.4 dynamic-slice.8
  873.9 29.5 %custom-call.28 = f32[3,128,128]{1,2,0:T(8,128)S(1)} custom-call(f32[3,128,128]{2,1,0:T(8,128)S(1)} %get-tuple-element.9), custom_call_target="InvertDiagBlocksLowerTriangular" | custom-call | tf_op jit(solution)/shard_map/jit(_cho_solve)/triangular_solve | solution.py:136
  (179 shorter events, 84.0 us)
Async XLA Ops:
  94.4 20.8 %copy-start.11 = (f32[12]{0:T(128)S(1)}, f32[12]{0:T(128)}, u32[]{:S(2)}) copy-start(f32[12]{0:T(128)} %constant.198) | copy-start | bytes 148
  94.4 20.8 %copy-start.10 = (f32[12]{0:T(128)S(1)}, f32[12]{0:T(128)}, u32[]{:S(2)}) copy-start(f32[12]{0:T(128)} %constant.200) | copy-start | bytes 148
  94.4 20.9 %copy-start.9 = (f32[12]{0:T(128)S(1)}, f32[12]{0:T(128)}, u32[]{:S(2)}) copy-start(f32[12]{0:T(128)} %constant.202) | copy-start | bytes 148
  94.4 21.2 %copy-start.3 = (f32[6,3,66]{2,1,0:T(4,128)S(1)}, f32[6,3,66]{2,1,0:T(4,128)}, u32[]{:S(2)}) copy-start(f32[6,3,66]{2,1,0:T(4,128)} %param.14) | copy-start | bytes 14260
  94.4 23.2 %copy-start.4 = (f32[3,21]{1,0:T(4,128)S(1)}, f32[3,21]{1,0:T(4,128)}, u32[]{:S(2)}) copy-start(f32[3,21]{1,0:T(4,128)} %param.15) | copy-start | bytes 760
  94.4 23.3 %copy-start.12 = (s32[21]{0:T(128)S(1)}, s32[21]{0:T(128)}, u32[]{:S(2)}) copy-start(s32[21]{0:T(128)} %param.18) | copy-start | bytes 256
  94.4 23.3 %copy-start.6 = (f32[21,3]{0,1:T(4,128)S(1)}, f32[21,3]{0,1:T(4,128)}, u32[]{:S(2)}) copy-start(f32[21,3]{0,1:T(4,128)} %param.20) | copy-start | bytes 760
  94.4 23.3 %copy-start.7 = (f32[21,3]{0,1:T(4,128)S(1)}, f32[21,3]{0,1:T(4,128)}, u32[]{:S(2)}) copy-start(f32[21,3]{0,1:T(4,128)} %param.19) | copy-start | bytes 760
  94.4 23.3 %copy-start.5 = (s32[6,66]{1,0:T(8,128)S(1)}, s32[6,66]{1,0:T(8,128)}, u32[]{:S(2)}) copy-start(s32[6,66]{1,0:T(8,128)} %param.17) | copy-start | bytes 4756
  94.4 23.7 %copy-start.1 = (f32[6,21,66,12]{2,1,3,0:T(8,128)S(1)}, f32[6,21,66,12]{2,1,3,0:T(8,128)}, u32[]{:S(2)}) copy-start(f32[6,21,66,12]{2,1,3,0:T(8,128)} %param.16) | copy-start | bytes 1197508
  94.4 214.3 %all-to-all-start = ((f32[64,6,1024]{2,1,0:T(8,128)}), f32[64,6,1024]{2,1,0:T(8,128)S(1)}, u32[]{:S(2)}, u32[]{:S(2)}) async-start(f32[64,6,1024]{2,1,0:T(8,128)} %constant_dynamic-update-slice_fusion), calls=%async_computation | async-start | bytes 4194304 | tf_op jit(solution)/shard_map/all_to_all | solution.py:16
  113.9 5.1 copy-start.8
  113.9 691.6 %all-reduce.4.cloned.1.call-start = ((), (), s32[]{:S(2)}) async-start(), calls=%async_computation.1 | async-start | bytes 1179648 | tf_op jit(solution)/shard_map/psum | solution.py:92
  312.1 3.5 copy-start.2
  805.5 1.4 copy-start
Sparse Core Ops, SparseCore 0:
  315.7 489.7 all-reduce.3
